TPU v7x, 512 devices: a whole 4x8x8 slice. The times are simulated.
512 devices in a mesh: param: 128 (over y, x_lo, z), ex: 4 (over x_hi, core).
Axes of the slice: x: 4 (x_hi: 2, x_lo: 2; x = x_hi * 2 + x_lo), y: 8, z: 8, core: 2. Of those that a mesh axis runs over, the one named last changes fastest.
Arguments:
- inputs: bfloat16 [4, 256, 8192], P('ex', 'param'), may hold values from -6 to 6
- cotangents: bfloat16 [4, 256, 16384], P('ex', None, 'param'), may hold values from -0.375 to 0.375
- sign_flips: bfloat16 [16384, 8192], P('param'), may hold values from -1 to 1, as said below
- sample_rows: int32 [8192], replicated, may hold values from 0 to 16383
- sample_columns: int32 [8192], replicated, may hold values from 0 to 8191
Outputs:
- sketch: float32 [4, 8192], P('ex', 'param')
Inputs may be any that keep to these rules, and one draw needn't show every extreme that they name: `sign_flips`: every entry is +1 or -1.
All inputs are finite; a program needn't handle non-finite values.
Results may differ from a plain program's by a relative error of at most 0.0003.
Values may be sent and summed in bfloat16 or wider, within the bound.
No kernel may reach another device: no remote copies, remote signals or barrier semaphores. Data moves between devices by JAX's collectives and lax.ppermute only.
A program may use at most 64 MiB of HBM per device.

v0:
```python
import math

import jax
import jax.numpy as jnp
from jax import lax
from jax.sharding import PartitionSpec as P


def hadamard_table(order):
    positions = lax.iota(jnp.int32, order)
    shared = jnp.bitwise_and(positions[:, None], positions[None, :])
    parity = jnp.zeros((order, order), jnp.int32)
    for bit_place in range(order.bit_length() - 1):
        parity = parity + jnp.bitwise_and(jnp.right_shift(shared, bit_place), 1)
    parity = parity % 2
    return (1.0 - 2.0 * parity).astype(jnp.float32)


def local_hadamard(vector):
    length = vector.shape[0]
    right_size = 1
    while right_size < length:
        block_size = min(128, length // right_size)
        left_size = length // (right_size * block_size)
        sign_table = hadamard_table(block_size)
        if right_size == 1:
            vector = jnp.dot(
                vector.reshape(left_size, block_size), sign_table, precision=lax.Precision.HIGHEST
            ).reshape(length)
        else:
            vector = jnp.einsum(
                "abc,bd->adc",
                vector.reshape(left_size, block_size, right_size),
                sign_table,
                precision=lax.Precision.HIGHEST,
            ).reshape(length)
        right_size *= block_size
    return vector


def shards(inputs, cotangents, sign_flips, sample_rows, sample_columns):
    part_count = lax.axis_size("param")
    own_index = lax.axis_index("param")
    activations = inputs[0]
    output_grad = cotangents[0]
    rows_here = output_grad.shape[1]
    model_width = activations.shape[1]
    block_length = rows_here * model_width
    norm_factor = 1.0 / math.sqrt(block_length * part_count)
    gradient = lax.dot_general(
        output_grad,
        lax.all_gather(activations, "param", axis=0, tiled=True),
        (((0,), (0,)), ((), ())),
        preferred_element_type=jnp.float32,
    )
    flipped = (gradient * sign_flips.astype(jnp.float32)).reshape(block_length)
    local_transform = local_hadamard(flipped)
    owner_block = sample_rows // rows_here
    offsets = sample_rows % rows_here * model_width + sample_columns
    device_table = hadamard_table(part_count)
    column_count = block_length // part_count
    mixed_columns = jnp.dot(
        device_table,
        lax.all_to_all(
            local_transform.reshape(part_count, column_count),
            "param",
            split_axis=0,
            concat_axis=0,
            tiled=True,
        ),
        precision=lax.Precision.HIGHEST,
    )
    owner_index = offsets // column_count
    column = offsets % column_count
    picked_values = mixed_columns[owner_block, column]
    contribution = jnp.where(owner_index == own_index, picked_values, 0.0)
    sketch_share = lax.psum_scatter(
        (contribution * norm_factor)[None, :], "param", scatter_dimension=1, tiled=True
    )
    return sketch_share


def solution(mesh):
    return jax.shard_map(
        shards,
        mesh=mesh,
        in_specs=(P("ex", "param", None), P("ex", None, "param"), P("param", None), P(), P()),
        out_specs=P("ex", "param"),
        check_vma=False,
    )
```

profile of v0, /device:TPU:4, one launch (start us, length us, event | category | flops | bytes accessed | tf_op | source)
XLA Modules:
  0.0 1500.5 jit_solution(17018038168457315414)
XLA Ops:
  6.5 0.0 copy-start
  6.5 0.0 all-gather.3.cloned.1.call-start
  6.5 1.5 copy.9
  8.0 0.0 all-gather.3.cloned.1.call-update
  8.0 637.6 %all-gather.3.cloned.1.call-done = bf16[1,256,8192]{2,0,1:T(2,128)(2,1)} async-done(((bf16[1,2,8192]{2,0,1:T(2,128)(2,1)}), bf16[1,256,8192]{2,0,1:T(2,128)(2,1)}) %all-gather.3.cloned.1.call-update) | async-done | bytes 4194320 | tf_op jit(solution)/shard_map/all_gather | solution.py:52
  645.7 0.0 copy-done
  645.7 10.9 convolution_multiply_fusion
  656.6 4.9 dot_general.18
  661.5 5.5 fusion.13
  666.9 4.1 fusion.15
  671.1 9.0 fusion
  680.1 7.7 all_to_all.11
  687.7 0.0 copy-start.1
  687.7 0.0 copy-start.2
  687.7 8.1 all-to-all-start
  695.9 0.0 reduce-scatter.4.cloned.1.call-start
  695.9 0.0 copy-done.1
  695.9 0.0 copy-done.2
  695.9 0.1 fusion.27
  696.0 52.9 %all-to-all-done = f32[128,1,8192]{2,1,0:T(1,128)} async-done(((f32[128,1,8192]{2,1,0:T(1,128)}), f32[128,1,8192]{2,1,0:T(1,128)}, u32[]{:S(2)}, u32[]{:S(2)}) %all-to-all-start) | async-done | bytes 4194336 | tf_op jit(solution)/shard_map/all_to_all | solution.py:64
  748.9 10.0 fusion.3
  758.9 99.8 %gather_fusion = f32[8192]{0:T(1024)S(1)} fusion(f32[128,8192]{1,0:T(8,128)} %fusion.3, s32[8192]{0:T(1024)S(1)} %fusion.27), kind=kCustom, calls=%fused_computation | custom fusion | bytes 131072 | tf_op jit(solution)/shard_map/gather | solution.py:75
  858.8 2.6 copy.14
  861.4 0.0 reduce-scatter.4.cloned.1.call-update
  861.4 630.9 %reduce-scatter.4.cloned.1.call-done = f32[64,1]{1,0:T(8,128)} async-done(((f32[8192,1]{1,0:T(8,128)}), f32[64,1]{1,0:T(8,128)}) %reduce-scatter.4.cloned.1.call-update) | async-done | bytes 272
  1492.3 1.3 copy.15
  (1 shorter events, 0.0 us)
Async XLA Ops:
  6.5 639.1 %copy-start = (bf16[1,256,128]{2,1,0:T(8,128)(2,1)S(1)}, bf16[1,256,128]{2,1,0:T(8,128)(2,1)}, u32[]{:S(2)}) copy-start(bf16[1,256,128]{2,1,0:T(8,128)(2,1)} %param.6) | copy-start | bytes 196612
  6.5 639.1 %all-gather.3.cloned.1.call-start = ((), (), s32[]{:S(2)}) async-start(), calls=%async_computation.2 | async-start | bytes 8454144 | tf_op jit(solution)/shard_map/all_gather | solution.py:52
  687.7 8.2 copy-start.1
  687.7 8.2 copy-start.2
  687.7 61.2 %all-to-all-start = ((f32[128,1,8192]{2,1,0:T(1,128)}), f32[128,1,8192]{2,1,0:T(1,128)}, u32[]{:S(2)}, u32[]{:S(2)}) async-start(f32[128,1,8192]{2,1,0:T(1,128)} %all_to_all.11), calls=%async_computation | async-start | bytes 8388608 | tf_op jit(solution)/shard_map/all_to_all | solution.py:64
  695.9 796.4 %reduce-scatter.4.cloned.1.call-start = ((), (), s32[]{:S(2)}) async-start(), calls=%async_computation.3 | async-start | bytes 4227072
Sparse Core Ops, SparseCore 0:
  9.4 636.2 all-gather.2
  861.5 630.6 reduce-scatter.3
where the time goes:
time: 1500 us
  waiting for transfers between devices  1320 us (88%)
  local copies, waits for them, and re-layouts  118 us (8%)
  matrix products  39.5 us (3%)
    all_gather x1, waiting for transfers between devices, shards(): lax.all_gather(activations, 'param', axis=0, tiled=True)  638 us
    unnamed x3, waiting for transfers between devices  631 us
    gather x1, local copies, waits for them, and re-layouts, shards(): picked_values = mixed_columns[owner_block, column]  99.8 us
    all_to_all x1, waiting for transfers between devices, shards(): lax.all_to_all(local_transform.reshape(part_count, column_count), 'param'...  52.9 us
  transfers between devices with their start and end apart: 3, of which 3 were waited for; matrix products, arithmetic and copies ran while one was open for 0% of the time, Pallas kernels for 0%

commit v1 on v0

v1 whole, which is shorter than its diff:
```python
import functools, math
import jax, jax.numpy as jnp
from jax import lax
from jax.sharding import PartitionSpec as P
from jax.experimental import pallas as pl
from jax.experimental.pallas import tpu as pltpu

def hadamard_table(order):
    p = lax.iota(jnp.int32, order)
    odd = lax.population_count(p[:, None] & p[None, :]) & 1
    return (1 - 2 * odd).astype(jnp.bfloat16)

def split(v):
    hi = v.astype(jnp.bfloat16)
    return hi, (v - hi.astype(jnp.float32)).astype(jnp.bfloat16)

def butterfly(parts):
    n = len(parts); s = 1
    parts = list(parts)
    while s < n:
        for i in range(n):
            if not i & s:
                a, b = parts[i], parts[i | s]
                parts[i], parts[i | s] = a + b, a - b
        s *= 2
    return parts

def kernel(norm, idx_ref, ct_ref, x_ref, s_ref, mt_ref, hr_ref, out_ref, t_ref, a0_ref, a1_ref):
    R, D = s_ref.shape
    L = 128
    CH = 8 * L
    nch = D // CH
    @pl.loop(0, nch)
    def _(c):
        cols = pl.ds(pl.multiple_of(c * CH, CH), CH)
        g = jnp.dot(ct_ref[...], x_ref[:, cols], preferred_element_type=jnp.float32)
        f = g * s_ref[:, cols].astype(jnp.float32)
        hi, lo = split(f)
        r = jnp.dot(hr_ref[...], jnp.concatenate([hi, lo], 0), preferred_element_type=jnp.float32)
        for t in range(R // 8):
            parts = butterfly([r[8*t:8*t+8, L*u:L*u+L] for u in range(8)])
            for u in range(8):
                t_ref[pl.ds(pl.multiple_of((c * 8 + u) * R + 8 * t, 8), 8), :] = parts[u]
    @pl.loop(0, R // 8)
    def _(t):
        for u in range(8):
            rows = [pl.ds(pl.multiple_of((8 * c + u) * R + 8 * t, 8), 8) for c in range(nch)]
            parts = butterfly([t_ref[w, :] for w in rows])
            for w, v in zip(rows, parts):
                t_ref[w, :] = v
    eye = lax.broadcasted_iota(jnp.int32, (L, L), 0) == lax.broadcasted_iota(jnp.int32, (L, L), 1)
    def gather(b, a_ref):
        for s in range(L):
            a_ref[pl.ds(s, 1), :] = t_ref[pl.ds(idx_ref[b * L + s], 1), :]
    def select(b, a_ref):
        hi, lo = split(a_ref[...])
        m = mt_ref[b]
        z = jnp.dot(jnp.concatenate([hi, lo], 1), jnp.concatenate([m, m], 0), preferred_element_type=jnp.float32)
        out_ref[pl.ds(b, 1), :] = jnp.sum(jnp.where(eye, z, 0.0), axis=0, keepdims=True) * norm
    nb = out_ref.shape[0]
    gather(0, a0_ref)
    @pl.loop(0, nb // 2)
    def _(i):
        b = 2 * i
        gather(b + 1, a1_ref)
        select(b, a0_ref)
        gather(jnp.minimum(b + 2, nb - 1), a0_ref)
        select(b + 1, a1_ref)

def local_call(idx, ct, x, s, mt, norm):
    R, D = s.shape
    n = idx.shape[0]
    h = hadamard_table(R)
    hr = jnp.concatenate([h, h], 1)
    vm = pl.BlockSpec(memory_space=pltpu.VMEM)
    return pl.pallas_call(
        functools.partial(kernel, norm),
        out_shape=jax.ShapeDtypeStruct((n // 128, 128), jnp.float32),
        in_specs=[pl.BlockSpec(memory_space=pltpu.SMEM)] + [vm] * 5,
        out_specs=vm,
        scratch_shapes=[pltpu.VMEM((R * D // 128, 128), jnp.float32), pltpu.VMEM((128, 128), jnp.float32), pltpu.VMEM((128, 128), jnp.float32)],
        compiler_params=pltpu.CompilerParams(vmem_limit_bytes=48 << 20),
    )(idx, ct, x, s, mt, hr)

def tables(rows, cols, R, p):
    idx = (cols // 128) * R + rows % R
    lane = cols % 128
    n = rows.shape[0]
    par = lax.population_count(rows // R & p) & 1
    l = lax.iota(jnp.int32, 128)
    odd = (lax.population_count(l[None, :, None] & lane.reshape(-1, 1, 128)) + par.reshape(-1, 1, 128)) & 1
    return idx, (1 - 2 * odd).astype(jnp.bfloat16)


def shards(inputs, cotangents, sign_flips, sample_rows, sample_columns):
    own = lax.axis_index("param")
    parts = lax.axis_size("param")
    zs, xs = 8, 2
    ys = parts // (zs * xs)
    device = lambda y, x, z: (y * xs + x) * zs + z
    every = [(y, x, z) for y in range(ys) for x in range(xs) for z in range(zs)]
    across = [(device(y, x, z), device(y, 1 - x, z)) for y, x, z in every]
    planes = [[device(y, x, z) for y in range(ys) for z in range(zs)] for x in range(xs)]
    rows_here, width = sign_flips.shape
    norm = 1.0 / math.sqrt(parts * rows_here * width)
    tokens = inputs[0]
    other = lax.ppermute(tokens, "param", across)
    gathered = lax.all_gather(
        jnp.concatenate([tokens, other], 0), "param", axis=0, tiled=True, axis_index_groups=planes
    )
    mine = own // zs % xs
    grad = cotangents[0].reshape(ys, xs, zs, -1, rows_here)
    grad = jnp.where(mine == 0, grad, grad[:, ::-1]).transpose(0, 2, 1, 3, 4).reshape(-1, rows_here)
    index, table = tables(sample_rows, sample_columns, rows_here, own)
    picked = local_call(index, grad.T, gathered, sign_flips, table, norm)
    pair = picked.reshape(parts, 1, -1)
    return lax.all_to_all(pair, "param", 0, 0, tiled=True).sum(0)


def solution(mesh):
    return jax.shard_map(
        shards,
        mesh=mesh,
        in_specs=(P("ex", "param", None), P("ex", None, "param"), P("param", None), P(), P()),
        out_specs=P("ex", "param"),
        check_vma=False,
    )
```

time: 1500 us -> 161 us (0.11)
  waiting for transfers between devices: 1320 us -> 91.4 us
  local copies, waits for them, and re-layouts: 118 us -> 9.6 us
  matrix products: 39.5 us -> 0 us
  blocking collectives: 0 us -> 22.6 us
  Pallas kernels: 0 us -> 15.8 us
    unnamed x3 -> x1, waiting for transfers between devices: 631 us -> 0.02 us
    all_gather x1, waiting for transfers between devices: 638 us -> 88.5 us  [shards(): lax.all_gather(jnp.concatenate([tokens, other], 0), 'param', axis=0, tile...]
    gather x1 -> x0, local copies, waits for them, and re-layouts: 99.8 us -> none  [shards(): picked_values = mixed_columns[owner_block, column]]
    all_to_all x1 -> x0, waiting for transfers between devices: 52.9 us -> none  [shards(): lax.all_to_all(local_transform.reshape(part_count, column_count), 'param'...]
    dot_general x5 -> x0, matrix products: 39.5 us -> none  [the longest x2 13.1 us: local_hadamard(): jnp.einsum('abc,bd->adc', vector.reshape(left_size, block_size, right_siz...]
    all_to_all x0 -> x1, blocking collectives: none -> 22.6 us  [shards(): return lax.all_to_all(pair, 'param', 0, 0, tiled=True).sum(0)]
    pallas_call x0 -> x1, Pallas kernels: none -> 15.8 us  [local_call(): pl.pallas_call(functools.partial(kernel, norm), out_shape=jax.ShapeDtypeS...]
  transfers between devices with their start and end apart: 3 -> 2, of which waited for: 3 -> 2; matrix products, arithmetic and copies ran while one was open for 0% -> 2% of each run, Pallas kernels for 0% -> 0%
where the time goes in v1:
time: 161 us; the launch traced here: 160 us
  waiting for transfers between devices  91.4 us (57%)
  blocking collectives  22.6 us (14%)
  Pallas kernels  15.8 us (10%)
  between operations  13.5 us (8%)
  local copies, waits for them, and re-layouts  9.6 us (6%)
  other arithmetic  4.15 us (3%)
  starting transfers between devices  3.1 us (2%)
    all_gather x1, waiting for transfers between devices, shards(): lax.all_gather(jnp.concatenate([tokens, other], 0), 'param', axis=0, tile...  88.5 us
    all_to_all x1, blocking collectives, shards(): return lax.all_to_all(pair, 'param', 0, 0, tiled=True).sum(0)  22.6 us
    pallas_call x1, Pallas kernels, local_call(): pl.pallas_call(functools.partial(kernel, norm), out_shape=jax.ShapeDtypeS...  15.8 us
    unnamed x3, local copies, waits for them, and re-layouts  8.53 us
  transfers between devices with their start and end apart: 2, of which 2 were waited for; matrix products, arithmetic and copies ran while one was open for 2% of the time, Pallas kernels for 0%

profile of v1, /device:TPU:4, one launch (start us, length us, event | category | flops | bytes accessed | tf_op | source)
XLA Modules:
  0.0 160.1 jit_solution(18435162281999171656)
XLA Ops:
  6.5 0.0 all-gather.3.cloned.1.call-start
  6.5 3.1 %collective-permute-start = (bf16[2,8192]{1,0:T(2,128)(2,1)}, bf16[2,8192]{1,0:T(2,128)(2,1)S(1)}, u32[]{:S(2)}, u32[]{:S(2)}) collective-permute-start(bf16[2,8192]{1,0:T(2,128)(2,1)} %bitcast.18), channel_id=1, source_target_pairs={{0,32},{4,36},{8,40},{12,44},{16,48},{20,52},{24,56},{28,60},{32,0... | collective-permute-start | bytes 98312 | tf_op jit(solution)/shard_map/ppermute | solution.py:107
  9.6 2.9 %collective-permute-done = bf16[2,8192]{1,0:T(2,128)(2,1)S(1)} collective-permute-done((bf16[2,8192]{1,0:T(2,128)(2,1)}, bf16[2,8192]{1,0:T(2,128)(2,1)S(1)}, u32[]{:S(2)}, u32[]{:S(2)}) %collective-permute-start) | collective-permute-done | bytes 32800 | tf_op jit(solution)/shard_map/ppermute | solution.py:107
  12.5 1.4 maximum_bitcast_fusion
  14.0 0.0 all-gather.3.cloned.1.call-update
  14.0 0.9 copy.12
  14.9 0.1 broadcast_select_fusion
  15.0 0.1 copy.13
  15.2 0.8 fusion.2
  16.0 1.1 subtract_convert_fusion.mt_ref
  17.1 88.5 %all-gather.3.cloned.1.call-done = bf16[64,4,8192]{2,1,0:T(4,128)(2,1)} async-done(((bf16[1,4,8192]{2,1,0:T(4,128)(2,1)}), bf16[64,4,8192]{2,1,0:T(4,128)(2,1)}) %all-gather.3.cloned.1.call-update) | async-done | bytes 4194320 | tf_op jit(solution)/shard_map/all_gather | solution.py:108
  105.6 6.9 %reshape.14.x_ref = bf16[256,8192]{1,0:T(8,128)(2,1)} reshape(bf16[64,4,8192]{2,1,0:T(4,128)(2,1)} %all-gather.3.cloned.1.call-done) | data formatting | bytes 8388608
  112.5 0.0 copy-start
  112.5 1.6 copy-done
  114.1 15.8 %shard_map.55 = f32[64,128]{1,0:T(8,128)S(1)} custom-call(s32[8192]{0:T(1024)S(1)} %get-tuple-element.6.idx_ref, bf16[128,256]{1,0:T(8,128)(2,1)S(1)} %bitcast.14, bf16[256,8192]{1,0:T(8,128)(2,1)} %reshape.14.x_ref, bf16[128,8192]{1,0:T(8,128)(2,1)S(1)} %copy-done, bf16[64,128,128]{2,1,0:T(8,128)(2,1)S(1)} %subtract_convert_fusion.mt_ref, ...), custom_call_target="tpu_custom_call" | custom-call | tf_op jit(solution)/shard_map/pallas_call | solution.py:76
  129.9 0.1 reshape.12
  130.0 22.6 %all_to_all.5 = f32[128,1,64]{2,1,0:T(1,128)S(1)} all-to-all(f32[128,1,64]{2,1,0:T(1,128)S(1)} %bitcast.16), channel_id=1, replica_groups=mesh['param'=128,'ex'=4] {'param'}, dimensions={0} | all-to-all | bytes 65536 | tf_op jit(solution)/shard_map/all_to_all | solution.py:117
  152.6 0.7 reduce_sum.11
  (2 shorter events, 0.0 us)
Async XLA Ops:
  6.5 99.1 %all-gather.3.cloned.1.call-start = ((), (), s32[]{:S(2)}) async-start(), calls=%async_computation.1 | async-start | bytes 4259840 | tf_op jit(solution)/shard_map/all_gather | solution.py:108
  6.5 6.0 %collective-permute-start = (bf16[2,8192]{1,0:T(2,128)(2,1)}, bf16[2,8192]{1,0:T(2,128)(2,1)S(1)}, u32[]{:S(2)}, u32[]{:S(2)}) collective-permute-start(bf16[2,8192]{1,0:T(2,128)(2,1)} %bitcast.18), channel_id=1, source_target_pairs={{0,32},{4,36},{8,40},{12,44},{16,48},{20,52},{24,56},{28,60},{32,0... | collective-permute-start | bytes 98312 | tf_op jit(solution)/shard_map/ppermute | solution.py:107
  112.5 1.6 copy-start
Sparse Core Ops, SparseCore 0:
  14.1 91.4 all-gather.2
